TPU v7x, 32 devices: a whole 2x2x4 slice. The times are simulated.
32 devices in a mesh: groups: 2 (over y), img: 4 (over z), ref: 2 (over x), rep: 2 (over core).
Axes of the slice: x: 2, y: 2, z: 4, core: 2. Of those that a mesh axis runs over, the one named last changes fastest.
Arguments:
- images: float32 [768, 4096], P(('groups', 'img')), parts along dimension 0, may hold values from -24 to 24
- references: float32 [4096, 2048], P('img', ('groups', 'ref', 'rep')), parts along dimension 1, may hold values from -1.2 to 1.2
- rotations: int32 [2048], P(('groups', 'ref', 'rep')), parts along dimension 0, may hold values from 0 to 7
- image_group: int32 [768], P(('groups', 'img')), parts along dimension 0, may hold values from 0 to 15
- noise_var: float32 [16], replicated, may hold values from 0.5 to 2
Outputs:
- class_means: float32 [4096, 2048], P('img', ('groups', 'ref', 'rep')), parts along dimension 1
- class_weights: float32 [2048], P(('groups', 'ref', 'rep')), parts along dimension 0
- log_evidence: float32 [768], P(('groups', 'img')), parts along dimension 0
There are 2 independent parts, one for each index of `groups`. A program takes and returns all parts, laid end to end along the dimension named above; an argument that names none is the same for every part. Nothing has to cross between parts.
All inputs are finite; a program needn't handle non-finite values.
Results may differ from a plain program's by a relative error of at most 0.0003.
Values sent between devices are 32-bit elements; how exact they have to be, the bound alone decides.
A program may use at most 64 MiB of HBM per device.

v0:
```python
import jax
import jax.numpy as jnp
from jax import lax
from jax.sharding import PartitionSpec as P

IMAGE_SIDE = 64
PIXELS = 4096


def joined(part, axis, combine):
    gathered = jax.tree.map(lambda a: lax.all_gather(a, axis), part)

    def take(source):
        return jax.tree.map(lambda a: lax.dynamic_index_in_dim(a, source, 0, False), gathered)

    return lax.fori_loop(
        1, lax.axis_size(axis), lambda source, state: combine(state, take(source)), take(0)
    )


def turn_forward(field, which):
    quarter = which % 4
    base = field if which < 4 else jnp.swapaxes(field, 0, 1)
    return jnp.rot90(base, quarter, axes=(0, 1))


def turn_inverse(field, which):
    quarter = which % 4
    base = jnp.rot90(field, -quarter, axes=(0, 1))
    return base if which < 4 else jnp.swapaxes(base, 0, 1)


def select_turn(field, rotations, turner):
    result = jnp.zeros_like(field)
    for which in range(8):
        result = jnp.where(rotations[None, None, :] == which, turner(field, which), result)
    return result


def combine_stats(first, second):
    top = jnp.maximum(first[0], second[0])
    total = first[1] * jnp.exp(first[0] - top) + second[1] * jnp.exp(second[0] - top)
    return (top, total)


def body(images, references, rotations, image_group, noise_var):
    gathered = lax.all_gather(references, "img", axis=0, tiled=True)
    rotated = select_turn(
        gathered.reshape(IMAGE_SIDE, IMAGE_SIDE, -1), rotations, turn_inverse
    ).reshape(PIXELS, -1)
    norms = jnp.sum(gathered * gathered, axis=0)
    group_hot = image_group[:, None] == jnp.arange(noise_var.shape[0])[None, :]
    sigma = jnp.sum(jnp.where(group_hot, noise_var[None, :], 0.0), axis=1)
    scores = (
        jnp.dot(
            images, rotated, precision=lax.Precision.HIGHEST, preferred_element_type=jnp.float32
        )
        - 0.5 * norms[None, :]
    ) / sigma[:, None]
    local_top = jnp.max(scores, axis=1)
    local_total = jnp.sum(jnp.exp(scores - local_top[:, None]), axis=1)
    top, total = joined((local_top, local_total), ("ref", "rep"), combine_stats)
    log_evidence = top + jnp.log(total)
    posterior = jnp.exp(scores - log_evidence[:, None])
    weight_sum = lax.psum(jnp.sum(posterior, axis=0), "img")
    numer_image = lax.dot_general(
        images,
        posterior,
        (((0,), (0,)), ((), ())),
        precision=lax.Precision.HIGHEST,
        preferred_element_type=jnp.float32,
    )
    numerator = select_turn(
        numer_image.reshape(IMAGE_SIDE, IMAGE_SIDE, -1), rotations, turn_forward
    ).reshape(PIXELS, -1)
    owned = lax.psum_scatter(numerator, "img", scatter_dimension=0, tiled=True)
    class_means = owned / (weight_sum + 1.0)[None, :]
    class_total = weight_sum.shape[0] * lax.axis_size("ref") * lax.axis_size("rep")
    image_total = images.shape[0] * lax.axis_size("img")
    class_weights = weight_sum * (class_total / image_total)
    return (class_means, class_weights, log_evidence)


def solution(mesh):
    placed = (
        P(("groups", "img"), None),
        P("img", ("groups", "ref", "rep")),
        P(("groups", "ref", "rep")),
        P(("groups", "img")),
        P(),
    )
    return jax.shard_map(
        body,
        mesh=mesh,
        in_specs=placed,
        out_specs=(
            P("img", ("groups", "ref", "rep")),
            P(("groups", "ref", "rep")),
            P(("groups", "img")),
        ),
        check_vma=False,
    )
```

profile of v0, /device:TPU:0, one launch (start us, length us, event | category | flops | bytes accessed | tf_op | source)
XLA Modules:
  0.0 286.7 jit_solution(2013551750306974672)
XLA Ops:
  7.2 0.7 all-gather.4.cloned.1.call-update
  8.0 1.2 dynamic-slice
  9.9 0.8 select_reduce_fusion
  10.6 0.7 broadcast_compare_fusion.7
  11.3 81.7 %all-gather.4.cloned.1.call-done = f32[4096,256]{1,0:T(8,128)} async-done(((f32[1024,256]{1,0:T(8,128)}), f32[4096,256]{1,0:T(8,128)}) %all-gather.4.cloned.1.call-update) | async-done | bytes 4194320 | tf_op jit(solution)/shard_map/all_gather | solution.py:47
  93.1 6.6 %rev.41 = f32[64,64,256]{2,1,0:T(8,128)} reverse(f32[64,64,256]{2,1,0:T(8,128)} %bitcast.41), dimensions={0,1} | reverse | bytes 8388608 | tf_op jit(solution)/shard_map/jit(rot90)/jit(_flip)/rev | solution.py:29
  99.7 6.7 %rev.40 = f32[64,64,256]{2,1,0:T(8,128)} reverse(f32[64,64,256]{2,1,0:T(8,128)} %bitcast.42), dimensions={1} | reverse | bytes 8388608 | tf_op jit(solution)/shard_map/jit(rot90)/jit(_flip)/rev | solution.py:29
  106.4 4.7 %rev.42 = f32[64,64,256]{2,0,1:T(8,128)} reverse(f32[64,64,256]{2,0,1:T(8,128)} %bitcast.43), dimensions={1} | reverse | bytes 8388608 | tf_op jit(solution)/shard_map/jit(rot90)/jit(_flip)/rev | solution.py:29
  111.0 2.9 %multiply_reduce_fusion = f32[256]{0:T(256)S(1)} fusion(f32[4096,256]{1,0:T(8,128)} %all-gather.4.cloned.1.call-done), kind=kLoop, calls=%fused_computation.22 | loop fusion | flops 2096896 | bytes 4195328 | tf_op jit(solution)/shard_map/reduce_sum | solution.py:51
  113.9 0.5 copy-done.1
  114.5 16.2 %fusion.3 = f32[64,64,256]{2,1,0:T(8,128)S(1)} fusion(f32[64,64,256]{2,1,0:T(8,128)} %rev.40, f32[64,64,256]{2,0,1:T(8,128)} %rev.42, f32[64,64,256]{2,0,1:T(8,128)} %bitcast.52, f32[64,64,256]{2,0,1:T(8,128)S(1)} %bitcast.45, f32[64,64,256]{2,0,1:T(8,128)} %bitcast.53, f32[64,64,256]{2,1,0:T(8,128)} %rev.41, f32[64,64,256]{2,1,0:T(8,128)S(1)} %bitcast.44, ...), kind=kLoop, calls=%fused_computation.9 | loop fusion | flops 8388608 | bytes 33556480 | tf_op jit(solution)/shard_map/jit(_where)/select_n | solution.py:36
  130.7 2.6 fusion.13
  133.3 0.2 exponential_reduce_fusion
  133.5 0.2 dynamic-update-slice
  133.7 0.2 dynamic-update-slice.1
  133.9 6.6 %all-reduce.2 = (f32[384]{0:T(512)S(1)}, f32[384]{0:T(512)S(1)}) all-reduce(f32[384]{0:T(512)S(1)} %dynamic-update-slice, f32[384]{0:T(512)S(1)} %dynamic-update-slice.1), channel_id=2, replica_groups=mesh['groups'=2,'img'=4,'ref'=2,'rep'=2] {'ref','rep'}, use_global_device_ids=true, to_apply=%add | all-reduce | flops 768 | bytes 6144
  140.5 0.1 reshape.48
  140.6 0.1 reshape.49
  140.7 0.1 while.17
  140.8 5.3 %convolution_bitcast_fusion = f32[4096,256]{0,1:T(8,128)} fusion(f32[96,4096]{1,0:T(8,128)S(1)} %copy-done, f32[256,96]{0,1:T(8,128)S(1)} %get-tuple-element.163, f32[96]{0:T(128)S(1)} %log_add_fusion), kind=kOutput, calls=%fused_computation.6 | convolution fusion | flops 1207984128 | bytes 5865856 | tf_op jit(solution)/shard_map/dot_general | solution.py:66
  146.1 5.6 %copy.31 = f32[4096,256]{1,0:T(8,128)} copy(f32[4096,256]{0,1:T(8,128)} %convolution_bitcast_fusion) | data formatting | bytes 8388608 | tf_op jit(solution)/shard_map/dot_general | solution.py:66
  151.7 6.6 %copy.64 = f32[64,64,256]{2,0,1:T(8,128)} copy(f32[64,64,256]{2,1,0:T(8,128)} %bitcast.46) | data formatting | bytes 8388608 | tf_op jit(solution)/shard_map/reshape | solution.py:74
  158.2 6.7 %rev.45 = f32[64,64,256]{2,1,0:T(8,128)} reverse(f32[64,64,256]{2,1,0:T(8,128)} %bitcast.54), dimensions={1} | reverse | bytes 8388608 | tf_op jit(solution)/shard_map/jit(rot90)/jit(_flip)/rev | solution.py:24
  164.9 6.7 %rev.44 = f32[64,64,256]{2,1,0:T(8,128)} reverse(f32[64,64,256]{2,1,0:T(8,128)} %bitcast.55), dimensions={0,1} | reverse | bytes 8388608 | tf_op jit(solution)/shard_map/jit(rot90)/jit(_flip)/rev | solution.py:24
  171.6 6.6 %rev.43 = f32[64,64,256]{2,1,0:T(8,128)} reverse(f32[64,64,256]{2,1,0:T(8,128)} %bitcast.47), dimensions={1} | reverse | bytes 8388608 | tf_op jit(solution)/shard_map/jit(rot90)/jit(_flip)/rev | solution.py:24
  178.2 6.6 %rev.46 = f32[64,64,256]{2,1,0:T(8,128)} reverse(f32[64,64,256]{2,1,0:T(8,128)} %bitcast.48), dimensions={0,1} | reverse | bytes 8388608 | tf_op jit(solution)/shard_map/jit(rot90)/jit(_flip)/rev | solution.py:24
  184.9 17.6 %fusion.5 = f32[64,64,256]{2,1,0:T(8,128)} fusion(f32[64,64,256]{2,1,0:T(8,128)} %rev.43, f32[64,64,256]{2,1,0:T(8,128)} %rev.44, f32[64,64,256]{2,0,1:T(8,128)} %bitcast.50, f32[64,64,256]{2,1,0:T(8,128)} %rev.45, f32[64,64,256]{2,1,0:T(8,128)} %rev.46, f32[64,64,256]{2,0,1:T(8,128)} %bitcast.51, f32[64,64,256]{2,1,0:T(8,128)} %bitcast.49, ...), kind=kLoop, calls=%fused_computation.12 | loop fusion | flops 8388608 | bytes 33556480 | tf_op jit(solution)/shard_map/jit(_where)/select_n | solution.py:36
  202.5 0.1 fusion.11
  202.6 9.8 %psum.7 = f32[256]{0:T(256)S(1)} all-reduce(f32[256]{0:T(256)S(1)} %fusion.11), channel_id=1, replica_groups=mesh['groups'=2,'img'=4,'ref'=2,'rep'=2] {'img'}, use_global_device_ids=true, to_apply=%region_8.9 | all-reduce | flops 256 | bytes 2048 | tf_op jit(solution)/shard_map/psum | solution.py:65
  212.4 0.6 broadcast_multiply_fusion
  212.9 64.6 %reduce-scatter.2.cloned.1.call-done = f32[1024,256]{1,0:T(8,128)} async-done(((f32[4096,256]{1,0:T(8,128)}), f32[1024,256]{1,0:T(8,128)}) %reduce-scatter.2.cloned.1.call-update) | async-done | bytes 1048592 | tf_op jit(solution)/shard_map/reduce_scatter | solution.py:76
  277.6 2.3 broadcast_divide_fusion
  (17 shorter events, 0.2 us)
Async XLA Ops:
  7.2 123.5 %copy-start = (f32[96,4096]{1,0:T(8,128)S(1)}, f32[96,4096]{1,0:T(8,128)}, u32[]{:S(2)}) copy-start(f32[96,4096]{1,0:T(8,128)} %param.7) | copy-start | bytes 4718596
  7.2 85.9 %all-gather.4.cloned.1.call-start = ((), (), s32[]{:S(2)}) async-start(), calls=%async_computation.1 | async-start | bytes 5242880 | tf_op jit(solution)/shard_map/all_gather | solution.py:47
  7.9 269.6 %reduce-scatter.2.cloned.1.call-start = ((), (), s32[]{:S(2)}) async-start(), calls=%async_computation.2 | async-start | bytes 5242880 | tf_op jit(solution)/shard_map/reduce_scatter | solution.py:76
  111.0 3.4 %copy-start.1 = (f32[4096,256]{1,0:T(8,128)S(1)}, f32[4096,256]{1,0:T(8,128)}, u32[]{:S(2)}) copy-start(f32[4096,256]{1,0:T(8,128)} %all-gather.4.cloned.1.call-done) | copy-start | bytes 12582916
  140.8 61.7 %copy-start.2 = (f32[96]{0:T(128)}, f32[96]{0:T(128)S(1)}, u32[]{:S(2)}) copy-start(f32[96]{0:T(128)S(1)} %log_add_fusion) | copy-start | bytes 1156
Sparse Core Ops, SparseCore 0:
  9.6 83.4 all-gather.3
  202.6 74.9 reduce-scatter.1
where the time goes:
time: 288 us; the launch traced here: 287 us
  waiting for transfers between devices  147 us (51%)
  local copies, waits for them, and re-layouts  59.2 us (21%)
  other arithmetic  41.3 us (14%)
  blocking collectives  16.3 us (6%)
  between operations  14.8 us (5%)
  matrix products  7.87 us (3%)
    all_gather x1, waiting for transfers between devices, body(): gathered = lax.all_gather(references, 'img', axis=0, tiled=True)  81.7 us
    reduce_scatter x1, waiting for transfers between devices, body(): owned = lax.psum_scatter(numerator, 'img', scatter_dimension=0, tiled=True)  64.6 us
    select_n x2, other arithmetic, select_turn(): jnp.where(rotations[None, None, :] == which, turner(field, which), result)  33.8 us
    rev x4, local copies, waits for them, and re-layouts, turn_forward(): return jnp.rot90(base, quarter, axes=(0, 1))  26.6 us
    rev x3, local copies, waits for them, and re-layouts, turn_inverse(): base = jnp.rot90(field, -quarter, axes=(0, 1))  18 us
    psum x1, blocking collectives, body(): weight_sum = lax.psum(jnp.sum(posterior, axis=0), 'img')  9.77 us
    reshape x1, local copies, waits for them, and re-layouts, body(): numer_image.reshape(IMAGE_SIDE, IMAGE_SIDE, -1)  6.57 us
    unnamed x1, blocking collectives  6.57 us
  transfers between devices with their start and end apart: 2, of which 2 were waited for; matrix products, arithmetic and copies ran while one was open for 1% of the time, Pallas kernels for 0%

commit v1 on v0

--- a/solution.py
+++ b/solution.py
@@ -1,10 +1,19 @@
+import functools
+
 import jax
 import jax.numpy as jnp
 from jax import lax
+from jax.experimental import pallas as pl
+from jax.experimental.pallas import tpu as pltpu
 from jax.sharding import PartitionSpec as P
 
 IMAGE_SIDE = 64
 PIXELS = 4096
+MESH = pl.DeviceIdType.MESH
+F32 = jnp.float32
+BF16 = jnp.bfloat16
+CHUNKS = 4
+LANES = 128
 
 
 def joined(part, axis, combine):
@@ -81,7 +90,358 @@
     return (class_means, class_weights, log_evidence)
 
 
+def halves(x):
+    high = x.astype(BF16)
+    return high, (x - high.astype(F32)).astype(BF16)
+
+
+def dot3(a, b, dims):
+    ah, al = halves(a)
+    bh, bl = halves(b)
+    one = lambda x, y: lax.dot_general(x, y, (dims, ((), ())), preferred_element_type=F32)
+    return one(ah, bh) + (one(ah, bl) + one(al, bh))
+
+
+def reverse_rows(x):
+    place = lax.broadcasted_iota(jnp.int32, (8, x.shape[1]), 0)
+    odd = place % 2 == 1
+    second = (place // 2) % 2 == 1
+    pieces = []
+    for g in reversed(range(x.shape[0] // 8)):
+        p = x[8 * g : 8 * g + 8]
+        p = jnp.where(odd, pltpu.roll(p, 1, 0), pltpu.roll(p, 7, 0))
+        p = jnp.where(second, pltpu.roll(p, 2, 0), pltpu.roll(p, 6, 0))
+        pieces.append(pltpu.roll(p, 4, 0))
+    return jnp.concatenate(pieces, axis=0)
+
+
+def kernel(
+    zs,
+    images_ref, refs_ref, rot_ref, sigma_ref,
+    means_ref, weights_ref, evidence_ref,
+    full, wide, scores, parts, stats, posts, num,
+    load_sem, z_recv, x_recv, c_recv, cx_recv,
+    right_send, left_send, x_send, c_send, cx_send,
+    s_send, s_recv, t_send, t_recv, p_send, p_recv,
+):
+    z = lax.axis_index("img")
+    x = lax.axis_index("ref")
+    c = lax.axis_index("rep")
+    rows = images_ref.shape[0]
+    classes = refs_ref.shape[1]
+    quarter = rows // 4
+    strip = PIXELS // CHUNKS
+    side = IMAGE_SIDE
+    own_lines = side // zs
+    others = [{"ref": 1 - x}, {"rep": 1 - c}, {"ref": 1 - x, "rep": 1 - c}]
+
+    barrier = pltpu.get_barrier_semaphore()
+    for d in range(1, zs):
+        pl.semaphore_signal(barrier, inc=1, device_id={"img": lax.rem(z + d, zs)}, device_id_type=MESH)
+    for where in others:
+        pl.semaphore_signal(barrier, inc=1, device_id=where, device_id_type=MESH)
+    pl.semaphore_wait(barrier, zs + 2)
+
+    def quarter_rows(xi, ci):
+        return pl.ds(pl.multiple_of((xi * 2 + ci) * quarter, 8), quarter)
+
+    def columns(chunk):
+        return pl.ds(pl.multiple_of(chunk * strip, strip), strip)
+
+    def send(src, dst, ssem, rsem, where):
+        return pltpu.make_async_remote_copy(
+            src_ref=src, dst_ref=dst, send_sem=ssem, recv_sem=rsem,
+            device_id=where, device_id_type=MESH,
+        )
+
+    def piece(src, chunk, xi, ci):
+        return full.at[src, quarter_rows(xi, ci), columns(chunk)]
+
+    def go_right(src, chunk, first=False):
+        a = images_ref.at[quarter_rows(x, c), columns(chunk)] if first else piece(src, chunk, x, c)
+        return send(a, piece(src, chunk, x, c), right_send.at[src, chunk], z_recv.at[src, chunk], {"img": lax.rem(z + 1, zs)})
+
+    def go_left(src, chunk, first=False):
+        a = images_ref.at[quarter_rows(x, c), columns(chunk)] if first else piece(src, chunk, x, c)
+        return send(a, piece(src, chunk, x, c), left_send.at[src, chunk], z_recv.at[src, chunk], {"img": lax.rem(z + zs - 1, zs)})
+
+    def go_x(src, chunk):
+        return send(piece(src, chunk, x, c), piece(src, chunk, x, c), x_send.at[src, chunk], x_recv.at[src, chunk], {"ref": 1 - x})
+
+    def go_c(src, chunk):
+        return send(piece(src, chunk, x, c), piece(src, chunk, x, c), c_send.at[src, chunk], c_recv.at[src, chunk], {"rep": 1 - c})
+
+    def go_cx(src, chunk):
+        return send(piece(src, chunk, 1 - x, c), piece(src, chunk, 1 - x, c), cx_send.at[src, chunk], cx_recv.at[src, chunk], {"rep": 1 - c})
+
+    def partial(src):
+        return send(scores.at[src], parts.at[z], s_send.at[src], s_recv.at[z], {"img": src})
+
+    load = pltpu.make_async_copy(images_ref, full.at[z], load_sem)
+    load.start()
+    for chunk in range(CHUNKS):
+        @pl.when(z < zs - 1)
+        def _():
+            go_right(z, chunk, True).start()
+
+        @pl.when(z > 0)
+        def _():
+            go_left(z, chunk, True).start()
+
+    rot = rot_ref[...]
+    is_row = (rot == 0) | (rot == 7)
+    is_row_up = (rot == 5) | (rot == 2)
+    is_col = (rot == 4) | (rot == 3)
+    is_col_up = (rot == 1) | (rot == 6)
+    flipped = (rot == 7) | (rot == 2) | (rot == 3) | (rot == 6)
+
+    def clear(i, _):
+        wide[:, pl.ds(pl.multiple_of(i * side, side), side), :] = jnp.zeros((classes // LANES, side, LANES), F32)
+        return 0
+
+    lax.fori_loop(0, side, clear, 0)
+
+    def lane(h):
+        return slice(h * LANES, (h + 1) * LANES)
+
+    def line(i):
+        return pl.ds(pl.multiple_of(i * side, side), side)
+
+    def turned(i):
+        field = refs_ref[line(i), :]
+        return jnp.where(flipped, reverse_rows(field), field)
+
+    def put_rows(i, norm):
+        raw = refs_ref[line(i), :]
+        field = turned(i)
+        up = jnp.where(is_row, field, 0.0)
+        down = jnp.where(is_row_up, field, 0.0)
+        for h in range(classes // LANES):
+            wide[h, line(z * own_lines + i), :] = up[:, lane(h)]
+            wide[h, line(side - 1 - z * own_lines - i), :] = down[:, lane(h)]
+        return norm + jnp.sum(raw * raw, axis=0, keepdims=True)
+
+    norm = lax.fori_loop(0, own_lines, put_rows, jnp.zeros((1, classes), F32))
+
+    def put_columns(i, _):
+        field = turned(i)
+        across = jnp.where(is_col, field, 0.0)
+        back = jnp.where(is_col_up, field, 0.0)
+        for h in range(classes // LANES):
+            at = pl.ds(z * own_lines + i, side, stride=side)
+            wide[h, at, :] = wide[h, at, :] + across[:, lane(h)]
+            at = pl.ds(side - 1 - z * own_lines - i, side, stride=side)
+            wide[h, at, :] = wide[h, at, :] + back[:, lane(h)]
+        return 0
+
+    lax.fori_loop(0, own_lines, put_columns, 0)
+
+    def multiply(src, chunk, width):
+        at = pl.ds(pl.multiple_of(chunk * width, width), width)
+        weight = jnp.concatenate([wide[h, at, :] for h in range(classes // LANES)], axis=1)
+        return jnp.dot(full[src, :, at], weight, precision=lax.Precision.HIGHEST, preferred_element_type=F32)
+
+    start = jnp.broadcast_to(-0.5 * norm, (rows, classes))
+    for src in range(zs):
+        scores[src] = start
+    load.wait()
+
+    def own_part(chunk, _):
+        scores[z] = scores[z] + multiply(z, chunk, strip)
+        return 0
+
+    lax.fori_loop(0, CHUNKS, own_part, 0)
+
+    units = (zs - 1) * CHUNKS
+
+    def each(n, action):
+        s = 1 + n // CHUNKS
+        chunk = lax.rem(n, CHUNKS)
+        good = (n >= 0) & (n < units)
+
+        @pl.when(good & (z - s >= 0))
+        def _():
+            action(z - s, chunk, True)
+
+        @pl.when(good & (z + s <= zs - 1))
+        def _():
+            action(z + s, chunk, False)
+
+    def take_z(src, chunk, rightward):
+        go_right(src, chunk).wait_recv()
+        if rightward:
+            @pl.when(z < zs - 1)
+            def _():
+                go_right(src, chunk).start()
+        else:
+            @pl.when(z > 0)
+            def _():
+                go_left(src, chunk).start()
+        go_x(src, chunk).start()
+        go_c(src, chunk).start()
+
+    def take_x(src, chunk, rightward):
+        go_x(src, chunk).wait_recv()
+        go_cx(src, chunk).start()
+
+    def take_all(src, chunk, rightward):
+        go_c(src, chunk).wait_recv()
+        go_cx(src, chunk).wait_recv()
+        scores[src] = scores[src] + multiply(src, chunk, strip)
+
+        @pl.when(chunk == CHUNKS - 1)
+        def _():
+            partial(src).start()
+
+    def unit(n, _):
+        each(n, take_z)
+        each(n - 1, take_x)
+        each(n - 2, take_all)
+        return 0
+
+    lax.fori_loop(0, units + 2, unit, 0)
+
+    total_score = scores[z]
+    for d in range(1, zs):
+        src = lax.rem(z + d, zs)
+        send(scores.at[src], parts.at[src], s_send.at[src], s_recv.at[src], {"img": src}).wait_recv()
+        total_score = total_score + parts[src]
+    total_score = total_score / sigma_ref[...]
+    top = jnp.max(total_score, axis=1, keepdims=True)
+    total = jnp.sum(jnp.exp(total_score - top), axis=1, keepdims=True)
+    place = lax.broadcasted_iota(jnp.int32, (rows, LANES), 1)
+    stats[3] = jnp.where(place < LANES // 2, top, total)
+    shares = [send(stats.at[3], stats.at[m], t_send.at[m], t_recv.at[m], where) for m, where in enumerate(others)]
+    for share in shares:
+        share.start()
+    for share in shares:
+        share.wait()
+    half = LANES // 2
+    best = top
+    for m in range(3):
+        best = jnp.maximum(best, stats[m, :, 0:1])
+    summed = total * jnp.exp(top - best)
+    for m in range(3):
+        summed = summed + stats[m, :, half : half + 1] * jnp.exp(stats[m, :, 0:1] - best)
+    evidence = best + jnp.log(summed)
+    evidence_ref[...] = evidence
+    posts[z] = jnp.exp(total_score - evidence)
+
+    def give(src):
+        return send(posts.at[z], posts.at[z], p_send.at[src], p_recv.at[z], {"img": src})
+
+    for d in range(1, zs):
+        give(lax.rem(z + d, zs)).start()
+    for d in range(1, zs):
+        src = lax.rem(z + d, zs)
+        send(posts.at[src], posts.at[src], p_send.at[src], p_recv.at[src], {"img": src}).wait_recv()
+
+    weight_sum = jnp.zeros((1, classes), F32)
+    for src in range(zs):
+        weight_sum = weight_sum + jnp.sum(posts[src], axis=0, keepdims=True)
+    weights_ref[...] = weight_sum
+    width = 512
+
+    def weigh(n, _):
+        at = pl.ds(pl.multiple_of(n * width, width), width)
+        block = full[:, :, at].reshape(zs * rows, width)
+        result = dot3(block, posts[...].reshape(zs * rows, classes), (((0,), (0,))))
+        for h in range(classes // LANES):
+            num[h, at, :] = result[:, lane(h)]
+        return 0
+
+    lax.fori_loop(0, PIXELS // width, weigh, 0)
+
+    scale = 1.0 / (weight_sum + 1.0)
+
+    def finish(i, _):
+        fields = []
+        for h in range(classes // LANES):
+            up = num[h, line(z * own_lines + i), :]
+            down = num[h, line(side - 1 - z * own_lines - i), :]
+            across = num[h, pl.ds(z * own_lines + i, side, stride=side), :]
+            back = num[h, pl.ds(side - 1 - z * own_lines - i, side, stride=side), :]
+            k = lane(h)
+            fields.append(jnp.where(is_row[:, k], up, jnp.where(is_row_up[:, k], down, jnp.where(is_col[:, k], across, back))))
+        field = jnp.concatenate(fields, axis=1)
+        means_ref[line(i), :] = jnp.where(flipped, reverse_rows(field), field) * scale
+        return 0
+
+    lax.fori_loop(0, own_lines, finish, 0)
+
+    def settle(src, chunk, rightward):
+        if rightward:
+            @pl.when(z < zs - 1)
+            def _():
+                go_right(src, chunk).wait_send()
+        else:
+            @pl.when(z > 0)
+            def _():
+                go_left(src, chunk).wait_send()
+        go_x(src, chunk).wait_send()
+        go_c(src, chunk).wait_send()
+        go_cx(src, chunk).wait_send()
+
+    def settle_unit(n, _):
+        each(n, settle)
+        return 0
+
+    lax.fori_loop(0, units, settle_unit, 0)
+    for chunk in range(CHUNKS):
+        @pl.when(z < zs - 1)
+        def _():
+            go_right(z, chunk, True).wait_send()
+
+        @pl.when(z > 0)
+        def _():
+            go_left(z, chunk, True).wait_send()
+    for d in range(1, zs):
+        src = lax.rem(z + d, zs)
+        partial(src).wait_send()
+        give(src).wait_send()
+
+
+def turned_images_body(zs, images, references, rotations, image_group, noise_var):
+    rows = images.shape[0]
+    pixels, classes = references.shape
+    group_hot = image_group[:, None] == jnp.arange(noise_var.shape[0])[None, :]
+    sigma = jnp.sum(jnp.where(group_hot, noise_var[None, :], 0.0), axis=1, keepdims=True)
+    dma = pltpu.SemaphoreType.DMA
+    vmem = pl.BlockSpec(memory_space=pltpu.VMEM)
+    many = dma((zs, CHUNKS))
+    means, weight_sum, evidence = pl.pallas_call(
+        functools.partial(kernel, zs),
+        name="class_step",
+        out_shape=(
+            jax.ShapeDtypeStruct((pixels, classes), F32),
+            jax.ShapeDtypeStruct((1, classes), F32),
+            jax.ShapeDtypeStruct((rows, 1), F32),
+        ),
+        in_specs=[pl.BlockSpec(memory_space=pl.ANY), vmem, vmem, vmem],
+        out_specs=(vmem, vmem, vmem),
+        scratch_shapes=[
+            pltpu.VMEM((zs, rows, PIXELS), F32),
+            pltpu.VMEM((classes // LANES, PIXELS, LANES), F32),
+            pltpu.VMEM((zs, rows, classes), F32),
+            pltpu.VMEM((zs, rows, classes), F32),
+            pltpu.VMEM((4, rows, LANES), F32),
+            pltpu.VMEM((zs, rows, classes), F32),
+            pltpu.VMEM((classes // LANES, PIXELS, LANES), F32),
+            dma, many, many, many, many, many, many, many, many, many,
+            dma((zs,)), dma((zs,)), dma((3,)), dma((3,)), dma((zs,)), dma((zs,)),
+        ],
+        compiler_params=pltpu.CompilerParams(
+            collective_id=0, has_side_effects=True, vmem_limit_bytes=48 * 1024 * 1024
+        ),
+    )(images, references, rotations[None, :], sigma)
+    weight_sum = weight_sum[0]
+    class_total = classes * lax.axis_size("ref") * lax.axis_size("rep")
+    image_total = rows * zs
+    return (means, weight_sum * (class_total / image_total), evidence[:, 0])
+
+
 def solution(mesh):
+    sizes = dict(mesh.shape)
     placed = (
         P(("groups", "img"), None),
         P("img", ("groups", "ref", "rep")),
@@ -89,8 +449,25 @@
         P(("groups", "img")),
         P(),
     )
+
+    def choose(images, references, rotations, image_group, noise_var):
+        zs = sizes["img"]
+        rows = images.shape[0]
+        fits = (
+            sizes["ref"] == 2
+            and sizes["rep"] == 2
+            and zs % 2 == 0
+            and rows % 32 == 0
+            and references.shape[1] % LANES == 0
+            and IMAGE_SIDE % zs == 0
+            and zs * rows * PIXELS * 4 <= 12 * 1024 * 1024
+        )
+        if fits:
+            return turned_images_body(zs, images, references, rotations, image_group, noise_var)
+        return body(images, references, rotations, image_group, noise_var)
+
     return jax.shard_map(
-        body,
+        choose,
         mesh=mesh,
         in_specs=placed,
         out_specs=(

time: 288 us -> 81.3 us (0.28)
  the two profiles are of different devices: /device:TPU:0 before, /device:TPU:28 now
where the time goes in v1:
time: 81.3 us; the launch traced here: 81.1 us
  Pallas kernels  74.1 us (91%)
  local copies, waits for them, and re-layouts  4.38 us (5%)
  other arithmetic  1.95 us (2%)
    pallas_call x1, Pallas kernels, turned_images_body(): pl.pallas_call(functools.partial(kernel, zs), name='class_step', out_shap...  74.1 us
    unnamed x7, local copies, waits for them, and re-layouts  4.28 us

profile of v1, /device:TPU:28, one launch (start us, length us, event | category | flops | bytes accessed | tf_op | source)
XLA Modules:
  0.0 81.1 jit_solution(6454517845183100117)
XLA Ops:
  0.6 0.8 select_reduce_fusion
  1.4 0.1 copy.10.sigma_ref
  1.5 0.0 copy-start
  1.5 1.4 %copy-done = f32[96,4096]{1,0:T(8,128)S(1)} copy-done((f32[96,4096]{1,0:T(8,128)S(1)}, f32[96,4096]{1,0:T(8,128)}, u32[]{:S(2)}) %copy-start) | copy-done | bytes 1572888
  2.9 0.0 copy-start.1
  2.9 1.2 %copy-done.1 = f32[1024,256]{1,0:T(8,128)S(1)} copy-done((f32[1024,256]{1,0:T(8,128)S(1)}, f32[1024,256]{1,0:T(8,128)}, u32[]{:S(2)}) %copy-start.1) | copy-done | bytes 1048600
  4.1 0.0 copy-start.2
  4.1 0.7 copy-done.2
  4.8 74.1 %class_step.1 = (f32[1024,256]{1,0:T(8,128)S(1)}, f32[1,256]{1,0:T(1,128)S(1)}, f32[96,1]{1,0:T(8,128)S(1)}) custom-call(f32[96,4096]{1,0:T(8,128)S(1)} %copy-done, f32[1024,256]{1,0:T(8,128)S(1)} %copy-done.1, s32[1,256]{1,0:T(1,128)S(1)} %bitcast.3, f32[96,1]{1,0:T(8,128)S(1)} %copy.10.sigma_ref), custom_call_target="tpu_custom_call" | custom-call | tf_op jit(solution)/shard_map/class_step/pallas_call | solution.py:412
  78.9 0.6 reduce
  79.5 0.6 broadcast_multiply_fusion
  80.1 1.0 %copy.12 = f32[1024,256]{1,0:T(8,128)} copy(f32[1024,256]{1,0:T(8,128)S(1)} %get-tuple-element.12) | data formatting | bytes 2097152
Async XLA Ops:
  1.5 1.4 %copy-start = (f32[96,4096]{1,0:T(8,128)S(1)}, f32[96,4096]{1,0:T(8,128)}, u32[]{:S(2)}) copy-start(f32[96,4096]{1,0:T(8,128)} %images_ref.1) | copy-start | bytes 4718596
  2.9 1.2 %copy-start.1 = (f32[1024,256]{1,0:T(8,128)S(1)}, f32[1024,256]{1,0:T(8,128)}, u32[]{:S(2)}) copy-start(f32[1024,256]{1,0:T(8,128)} %refs_ref.1) | copy-start | bytes 3145732
  4.1 0.7 copy-start.2

commit v2 on v1

--- a/solution.py
+++ b/solution.py
@@ -12,8 +12,9 @@
 MESH = pl.DeviceIdType.MESH
 F32 = jnp.float32
 BF16 = jnp.bfloat16
-CHUNKS = 4
+CHUNKS = 2
 LANES = 128
+VMEM_BYTES = 62 * 1024 * 1024
 
 
 def joined(part, axis, combine):
@@ -95,13 +96,6 @@
     return high, (x - high.astype(F32)).astype(BF16)
 
 
-def dot3(a, b, dims):
-    ah, al = halves(a)
-    bh, bl = halves(b)
-    one = lambda x, y: lax.dot_general(x, y, (dims, ((), ())), preferred_element_type=F32)
-    return one(ah, bh) + (one(ah, bl) + one(al, bh))
-
-
 def reverse_rows(x):
     place = lax.broadcasted_iota(jnp.int32, (8, x.shape[1]), 0)
     odd = place % 2 == 1
@@ -116,13 +110,13 @@
 
 
 def kernel(
-    zs,
-    images_ref, refs_ref, rot_ref, sigma_ref,
+    zs, weight_scale,
+    images_ref, source_ref, rot_ref, group_ref, noise_ref,
     means_ref, weights_ref, evidence_ref,
-    full, wide, scores, parts, stats, posts, num,
-    load_sem, z_recv, x_recv, c_recv, cx_recv,
-    right_send, left_send, x_send, c_send, cx_send,
-    s_send, s_recv, t_send, t_recv, p_send, p_recv,
+    full, wide, scores, parts, stats, posts, num, refs_ref, factors, tall_high, tall_low, post_high, post_low,
+    load_sem, refs_sem, z_recv, x_recv, cx_recv,
+    right_send, left_send, x_send, cx_send,
+    s_send, s_recv, t_send, t_recv, p_send, p_recv, f_send, f_recv,
 ):
     z = lax.axis_index("img")
     x = lax.axis_index("ref")
@@ -135,15 +129,32 @@
     own_lines = side // zs
     others = [{"ref": 1 - x}, {"rep": 1 - c}, {"ref": 1 - x, "rep": 1 - c}]
 
+    load_refs = pltpu.make_async_copy(source_ref, refs_ref, refs_sem)
+    load_refs.start()
+    loads = [
+        pltpu.make_async_copy(images_ref.at[:, chunk * strip : (chunk + 1) * strip], full.at[z, chunk], load_sem.at[chunk])
+        for chunk in range(CHUNKS)
+    ]
+    for load in loads:
+        load.start()
     barrier = pltpu.get_barrier_semaphore()
     for d in range(1, zs):
         pl.semaphore_signal(barrier, inc=1, device_id={"img": lax.rem(z + d, zs)}, device_id_type=MESH)
     for where in others:
         pl.semaphore_signal(barrier, inc=1, device_id=where, device_id_type=MESH)
+
+    def clear(i, _):
+        wide[:, pl.ds(pl.multiple_of(i * side, side), side), :] = jnp.zeros((classes // LANES, side, LANES), F32)
+        return 0
+
+    lax.fori_loop(0, side, clear, 0)
+    for src in range(zs):
+        post_high[src * LANES + rows : (src + 1) * LANES, :] = jnp.zeros((LANES - rows, classes), BF16)
+        post_low[src * LANES + rows : (src + 1) * LANES, :] = jnp.zeros((LANES - rows, classes), BF16)
     pl.semaphore_wait(barrier, zs + 2)
 
     def quarter_rows(xi, ci):
-        return pl.ds(pl.multiple_of((xi * 2 + ci) * quarter, 8), quarter)
+        return pl.ds(pl.multiple_of((ci * 2 + xi) * quarter, 8), quarter)
 
     def columns(chunk):
         return pl.ds(pl.multiple_of(chunk * strip, strip), strip)
@@ -155,7 +166,7 @@
         )
 
     def piece(src, chunk, xi, ci):
-        return full.at[src, quarter_rows(xi, ci), columns(chunk)]
+        return full.at[src, chunk, quarter_rows(xi, ci), :]
 
     def go_right(src, chunk, first=False):
         a = images_ref.at[quarter_rows(x, c), columns(chunk)] if first else piece(src, chunk, x, c)
@@ -168,17 +179,13 @@
     def go_x(src, chunk):
         return send(piece(src, chunk, x, c), piece(src, chunk, x, c), x_send.at[src, chunk], x_recv.at[src, chunk], {"ref": 1 - x})
 
-    def go_c(src, chunk):
-        return send(piece(src, chunk, x, c), piece(src, chunk, x, c), c_send.at[src, chunk], c_recv.at[src, chunk], {"rep": 1 - c})
-
     def go_cx(src, chunk):
-        return send(piece(src, chunk, 1 - x, c), piece(src, chunk, 1 - x, c), cx_send.at[src, chunk], cx_recv.at[src, chunk], {"rep": 1 - c})
+        pair = full.at[src, chunk, pl.ds(pl.multiple_of(c * 2 * quarter, 8), 2 * quarter), :]
+        return send(pair, pair, cx_send.at[src, chunk], cx_recv.at[src, chunk], {"rep": 1 - c})
 
     def partial(src):
         return send(scores.at[src], parts.at[z], s_send.at[src], s_recv.at[z], {"img": src})
 
-    load = pltpu.make_async_copy(images_ref, full.at[z], load_sem)
-    load.start()
     for chunk in range(CHUNKS):
         @pl.when(z < zs - 1)
         def _():
@@ -194,12 +201,6 @@
     is_col = (rot == 4) | (rot == 3)
     is_col_up = (rot == 1) | (rot == 6)
     flipped = (rot == 7) | (rot == 2) | (rot == 3) | (rot == 6)
-
-    def clear(i, _):
-        wide[:, pl.ds(pl.multiple_of(i * side, side), side), :] = jnp.zeros((classes // LANES, side, LANES), F32)
-        return 0
-
-    lax.fori_loop(0, side, clear, 0)
 
     def lane(h):
         return slice(h * LANES, (h + 1) * LANES)
@@ -220,8 +221,6 @@
             wide[h, line(z * own_lines + i), :] = up[:, lane(h)]
             wide[h, line(side - 1 - z * own_lines - i), :] = down[:, lane(h)]
         return norm + jnp.sum(raw * raw, axis=0, keepdims=True)
-
-    norm = lax.fori_loop(0, own_lines, put_rows, jnp.zeros((1, classes), F32))
 
     def put_columns(i, _):
         field = turned(i)
@@ -234,25 +233,35 @@
             wide[h, at, :] = wide[h, at, :] + back[:, lane(h)]
         return 0
 
-    lax.fori_loop(0, own_lines, put_columns, 0)
-
-    def multiply(src, chunk, width):
-        at = pl.ds(pl.multiple_of(chunk * width, width), width)
+    def multiply(src, chunk):
+        at = columns(chunk)
         weight = jnp.concatenate([wide[h, at, :] for h in range(classes // LANES)], axis=1)
-        return jnp.dot(full[src, :, at], weight, precision=lax.Precision.HIGHEST, preferred_element_type=F32)
-
-    start = jnp.broadcast_to(-0.5 * norm, (rows, classes))
-    for src in range(zs):
-        scores[src] = start
-    load.wait()
-
-    def own_part(chunk, _):
-        scores[z] = scores[z] + multiply(z, chunk, strip)
-        return 0
-
-    lax.fori_loop(0, CHUNKS, own_part, 0)
+        return jnp.dot(full[src, chunk], weight, precision=lax.Precision.HIGHEST, preferred_element_type=F32)
+
+    def keep(src, chunk):
+        block = full[src, chunk]
+        if rows < LANES:
+            block = jnp.concatenate([block, jnp.zeros((LANES - rows, strip), F32)], axis=0)
+        high, low = halves(block.T)
+        at = pl.ds(pl.multiple_of(src * LANES, LANES), LANES)
+        tall_high[columns(chunk), at] = high
+        tall_low[columns(chunk), at] = low
+
+    def prepare_rows():
+        load_refs.wait()
+        norm = lax.fori_loop(0, own_lines, put_rows, jnp.zeros((1, classes), F32))
+        start = jnp.broadcast_to(-0.5 * norm, (rows, classes))
+        for src in range(zs):
+            scores[src] = start
+        for load in loads:
+            load.wait()
+
+    def own_part(chunk):
+        scores[z] = scores[z] + multiply(z, chunk)
+        keep(z, chunk)
 
     units = (zs - 1) * CHUNKS
+    lead = max(CHUNKS, 4)
 
     def each(n, action):
         s = 1 + n // CHUNKS
@@ -278,16 +287,15 @@
             def _():
                 go_left(src, chunk).start()
         go_x(src, chunk).start()
-        go_c(src, chunk).start()
 
     def take_x(src, chunk, rightward):
         go_x(src, chunk).wait_recv()
         go_cx(src, chunk).start()
 
     def take_all(src, chunk, rightward):
-        go_c(src, chunk).wait_recv()
         go_cx(src, chunk).wait_recv()
-        scores[src] = scores[src] + multiply(src, chunk, strip)
+        scores[src] = scores[src] + multiply(src, chunk)
+        keep(src, chunk)
 
         @pl.when(chunk == CHUNKS - 1)
         def _():
@@ -296,7 +304,25 @@
     def unit(n, _):
         each(n, take_z)
         each(n - 1, take_x)
-        each(n - 2, take_all)
+
+        @pl.when(n == 0)
+        def _():
+            prepare_rows()
+
+        @pl.when((n >= 1) & (n < lead // 2))
+        def _():
+            steps = lead // 2 - 1
+            lax.fori_loop((n - 1) * own_lines // steps, n * own_lines // steps, put_columns, 0)
+
+        for k in range(lead // 2, lead):
+            @pl.when(n == k)
+            def _():
+                share = CHUNKS * 2 // lead
+                for chunk in range((k - lead // 2) * share, (k - lead // 2 + 1) * share):
+                    own_part(chunk)
+
+        each(jnp.where(n < lead, -1, jnp.where(n < 2 * lead - 2, 2 * (n - lead), n - 2)), take_all)
+        each(jnp.where((n < lead) | (n >= 2 * lead - 2), -1, 2 * (n - lead) + 1), take_all)
         return 0
 
     lax.fori_loop(0, units + 2, unit, 0)
@@ -306,46 +332,76 @@
         src = lax.rem(z + d, zs)
         send(scores.at[src], parts.at[src], s_send.at[src], s_recv.at[src], {"img": src}).wait_recv()
         total_score = total_score + parts[src]
-    total_score = total_score / sigma_ref[...]
+    groups = group_ref[...]
+    sigma_row = jnp.zeros(groups.shape, F32)
+    for g in range(noise_ref.shape[1]):
+        sigma_row = jnp.where(groups == g, noise_ref[0:1, g : g + 1], sigma_row)
+
+    def upright(row):
+        return jnp.broadcast_to(row, (LANES, row.shape[1])).T[:, 0:1]
+
+    total_score = total_score / upright(sigma_row)
     top = jnp.max(total_score, axis=1, keepdims=True)
-    total = jnp.sum(jnp.exp(total_score - top), axis=1, keepdims=True)
+    shifted = jnp.exp(total_score - top)
+    posts[z] = shifted
+
+    def give(src):
+        return send(posts.at[z], posts.at[z], p_send.at[src], p_recv.at[z], {"img": src})
+
+    def give_factor(src):
+        return send(factors.at[z], factors.at[z], f_send.at[src], f_recv.at[z], {"img": src})
+
+    for d in range(1, zs):
+        give(lax.rem(z + d, zs)).start()
+    total = jnp.sum(shifted, axis=1, keepdims=True)
     place = lax.broadcasted_iota(jnp.int32, (rows, LANES), 1)
-    stats[3] = jnp.where(place < LANES // 2, top, total)
+    pair = jnp.where(place < LANES // 2, top, total)
+    if rows < LANES:
+        pair = jnp.concatenate([pair, jnp.ones((LANES - rows, LANES), F32)], axis=0)
+    pair = pair.T
+    tops, totals = pair[0:8], pair[LANES // 2 : LANES // 2 + 8]
+    stats[3, 0:8, :] = tops
+    stats[3, 8:16, :] = totals
     shares = [send(stats.at[3], stats.at[m], t_send.at[m], t_recv.at[m], where) for m, where in enumerate(others)]
     for share in shares:
         share.start()
     for share in shares:
         share.wait()
-    half = LANES // 2
-    best = top
+    best = tops
     for m in range(3):
-        best = jnp.maximum(best, stats[m, :, 0:1])
-    summed = total * jnp.exp(top - best)
+        best = jnp.maximum(best, stats[m, 0:8, :])
+    summed = totals * jnp.exp(tops - best)
     for m in range(3):
-        summed = summed + stats[m, :, half : half + 1] * jnp.exp(stats[m, :, 0:1] - best)
+        summed = summed + stats[m, 8:16, :] * jnp.exp(stats[m, 0:8, :] - best)
     evidence = best + jnp.log(summed)
-    evidence_ref[...] = evidence
-    posts[z] = jnp.exp(total_score - evidence)
-
-    def give(src):
-        return send(posts.at[z], posts.at[z], p_send.at[src], p_recv.at[z], {"img": src})
-
+    evidence_ref[...] = evidence[0:1, :rows]
+    factors[z] = jnp.exp(tops - evidence)
     for d in range(1, zs):
-        give(lax.rem(z + d, zs)).start()
+        give_factor(lax.rem(z + d, zs)).start()
+
+    def settle_posts(src, weight_sum):
+        factor = upright(factors[src, 0:1, :])[:rows]
+        post = posts[src] * factor
+        high, low = halves(post)
+        at = pl.ds(pl.multiple_of(src * LANES, LANES), rows)
+        post_high[at, :] = high
+        post_low[at, :] = low
+        return weight_sum + jnp.sum(post, axis=0, keepdims=True)
+
+    weight_sum = settle_posts(z, jnp.zeros((1, classes), F32))
     for d in range(1, zs):
         src = lax.rem(z + d, zs)
         send(posts.at[src], posts.at[src], p_send.at[src], p_recv.at[src], {"img": src}).wait_recv()
-
-    weight_sum = jnp.zeros((1, classes), F32)
-    for src in range(zs):
-        weight_sum = weight_sum + jnp.sum(posts[src], axis=0, keepdims=True)
-    weights_ref[...] = weight_sum
+        send(factors.at[src], factors.at[src], f_send.at[src], f_recv.at[src], {"img": src}).wait_recv()
+        weight_sum = settle_posts(src, weight_sum)
+    weights_ref[...] = weight_sum * weight_scale
     width = 512
 
     def weigh(n, _):
         at = pl.ds(pl.multiple_of(n * width, width), width)
-        block = full[:, :, at].reshape(zs * rows, width)
-        result = dot3(block, posts[...].reshape(zs * rows, classes), (((0,), (0,))))
+        ah, al, bh, bl = tall_high[at, :], tall_low[at, :], post_high[...], post_low[...]
+        one = lambda p, q: jnp.dot(p, q, preferred_element_type=F32)
+        result = one(ah, bh) + (one(ah, bl) + one(al, bh))
         for h in range(classes // LANES):
             num[h, at, :] = result[:, lane(h)]
         return 0
@@ -379,7 +435,6 @@
             def _():
                 go_left(src, chunk).wait_send()
         go_x(src, chunk).wait_send()
-        go_c(src, chunk).wait_send()
         go_cx(src, chunk).wait_send()
 
     def settle_unit(n, _):
@@ -399,45 +454,49 @@
         src = lax.rem(z + d, zs)
         partial(src).wait_send()
         give(src).wait_send()
+        give_factor(src).wait_send()
 
 
 def turned_images_body(zs, images, references, rotations, image_group, noise_var):
     rows = images.shape[0]
     pixels, classes = references.shape
-    group_hot = image_group[:, None] == jnp.arange(noise_var.shape[0])[None, :]
-    sigma = jnp.sum(jnp.where(group_hot, noise_var[None, :], 0.0), axis=1, keepdims=True)
+    class_total = classes * lax.axis_size("ref") * lax.axis_size("rep")
+    image_total = rows * zs
     dma = pltpu.SemaphoreType.DMA
     vmem = pl.BlockSpec(memory_space=pltpu.VMEM)
     many = dma((zs, CHUNKS))
     means, weight_sum, evidence = pl.pallas_call(
-        functools.partial(kernel, zs),
+        functools.partial(kernel, zs, class_total / image_total),
         name="class_step",
         out_shape=(
             jax.ShapeDtypeStruct((pixels, classes), F32),
             jax.ShapeDtypeStruct((1, classes), F32),
-            jax.ShapeDtypeStruct((rows, 1), F32),
+            jax.ShapeDtypeStruct((1, rows), F32),
         ),
-        in_specs=[pl.BlockSpec(memory_space=pl.ANY), vmem, vmem, vmem],
+        in_specs=[pl.BlockSpec(memory_space=pl.ANY), pl.BlockSpec(memory_space=pl.ANY), vmem, vmem, vmem],
         out_specs=(vmem, vmem, vmem),
         scratch_shapes=[
-            pltpu.VMEM((zs, rows, PIXELS), F32),
+            pltpu.VMEM((zs, CHUNKS, rows, PIXELS // CHUNKS), F32),
             pltpu.VMEM((classes // LANES, PIXELS, LANES), F32),
             pltpu.VMEM((zs, rows, classes), F32),
             pltpu.VMEM((zs, rows, classes), F32),
-            pltpu.VMEM((4, rows, LANES), F32),
+            pltpu.VMEM((4, 16, LANES), F32),
             pltpu.VMEM((zs, rows, classes), F32),
             pltpu.VMEM((classes // LANES, PIXELS, LANES), F32),
-            dma, many, many, many, many, many, many, many, many, many,
-            dma((zs,)), dma((zs,)), dma((3,)), dma((3,)), dma((zs,)), dma((zs,)),
+            pltpu.VMEM((pixels, classes), F32),
+            pltpu.VMEM((zs, 8, LANES), F32),
+            pltpu.VMEM((PIXELS, zs * LANES), BF16),
+            pltpu.VMEM((PIXELS, zs * LANES), BF16),
+            pltpu.VMEM((zs * LANES, classes), BF16),
+            pltpu.VMEM((zs * LANES, classes), BF16),
+            dma((CHUNKS,)), dma, many, many, many, many, many, many, many,
+            dma((zs,)), dma((zs,)), dma((3,)), dma((3,)), dma((zs,)), dma((zs,)), dma((zs,)), dma((zs,)),
         ],
         compiler_params=pltpu.CompilerParams(
-            collective_id=0, has_side_effects=True, vmem_limit_bytes=48 * 1024 * 1024
+            collective_id=0, has_side_effects=True, vmem_limit_bytes=VMEM_BYTES
         ),
-    )(images, references, rotations[None, :], sigma)
-    weight_sum = weight_sum[0]
-    class_total = classes * lax.axis_size("ref") * lax.axis_size("rep")
-    image_total = rows * zs
-    return (means, weight_sum * (class_total / image_total), evidence[:, 0])
+    )(images, references, rotations[None, :], image_group[None, :], noise_var[None, :])
+    return (means, weight_sum[0], evidence[0])
 
 
 def solution(mesh):
@@ -458,6 +517,8 @@
             and sizes["rep"] == 2
             and zs % 2 == 0
             and rows % 32 == 0
+            and rows <= LANES
+            and zs >= 4
             and references.shape[1] % LANES == 0
             and IMAGE_SIDE % zs == 0
             and zs * rows * PIXELS * 4 <= 12 * 1024 * 1024

time: 81.3 us -> 73.6 us (0.905)
  the two profiles are of different devices: /device:TPU:28 before, /device:TPU:0 now
where the time goes in v2:
time: 73.6 us; the launch traced here: 73.4 us
  Pallas kernels  69.4 us (94%)
  local copies, waits for them, and re-layouts  3.35 us (5%)
    pallas_call x1, Pallas kernels, turned_images_body(): pl.pallas_call(functools.partial(kernel, zs, class_total / image_total),...  69.4 us
    unnamed x7, local copies, waits for them, and re-layouts  3.35 us

profile of v2, /device:TPU:0, one launch (start us, length us, event | category | flops | bytes accessed | tf_op | source)
XLA Modules:
  0.0 73.4 jit_solution(4757030458261243308)
XLA Ops:
  0.6 69.4 %class_step.1 = (f32[1024,256]{1,0:T(8,128)}, f32[1,256]{1,0:T(1,128)}, f32[1,96]{1,0:T(1,128)}) custom-call(f32[96,4096]{1,0:T(8,128)} %images_ref.1, f32[1024,256]{1,0:T(8,128)} %source_ref.1, s32[1,256]{1,0:T(1,128)} %bitcast.5, s32[1,96]{1,0:T(1,128)} %bitcast.7, f32[1,16]{1,0:T(1,128)} %bitcast.8), custom_call_target="tpu_custom_call" | custom-call | tf_op jit(solution)/shard_map/class_step/pallas_call | solution.py:468
  70.1 0.0 copy-start
  70.1 0.0 copy-start.1
  70.1 2.3 %copy.11 = f32[1024,256]{1,0:T(8,128)} copy(f32[1024,256]{1,0:T(8,128)} %get-tuple-element.12) | data formatting | bytes 2097152
  72.3 0.0 copy-done
  72.3 0.6 copy.12
  72.9 0.0 copy-done.1
  72.9 0.5 copy.13
Async XLA Ops:
  70.1 2.3 %copy-start = (f32[1,256]{1,0:T(1,128)S(1)}, f32[1,256]{1,0:T(1,128)}, u32[]{:S(2)}) copy-start(f32[1,256]{1,0:T(1,128)} %get-tuple-element.7) | copy-start | bytes 3076
  70.1 2.8 %copy-start.1 = (f32[1,96]{1,0:T(1,128)S(1)}, f32[1,96]{1,0:T(1,128)}, u32[]{:S(2)}) copy-start(f32[1,96]{1,0:T(1,128)} %get-tuple-element.8) | copy-start | bytes 1156

commit v3 on v2

--- a/solution.py
+++ b/solution.py
@@ -395,7 +395,7 @@
         send(factors.at[src], factors.at[src], f_send.at[src], f_recv.at[src], {"img": src}).wait_recv()
         weight_sum = settle_posts(src, weight_sum)
     weights_ref[...] = weight_sum * weight_scale
-    width = 512
+    width = 1024
 
     def weigh(n, _):
         at = pl.ds(pl.multiple_of(n * width, width), width)
@@ -423,7 +423,7 @@
         means_ref[line(i), :] = jnp.where(flipped, reverse_rows(field), field) * scale
         return 0
 
-    lax.fori_loop(0, own_lines, finish, 0)
+    lax.fori_loop(0, own_lines, finish, 0, unroll=2)
 
     def settle(src, chunk, rightward):
         if rightward:

time: 73.6 us -> 72.5 us (0.985)
  Pallas kernels: 69.4 us -> 68.3 us
    pallas_call x1, Pallas kernels: 69.4 us -> 68.3 us  [turned_images_body(): pl.pallas_call(functools.partial(kernel, zs, class_total / image_total),...]
where the time goes in v3:
time: 72.5 us; the launch traced here: 72.3 us
  Pallas kernels  68.3 us (94%)
  local copies, waits for them, and re-layouts  3.35 us (5%)
    pallas_call x1, Pallas kernels, turned_images_body(): pl.pallas_call(functools.partial(kernel, zs, class_total / image_total),...  68.3 us
    unnamed x7, local copies, waits for them, and re-layouts  3.35 us

profile of v3, /device:TPU:0, one launch (start us, length us, event | category | flops | bytes accessed | tf_op | source)
XLA Modules:
  0.0 72.3 jit_solution(4177562836491543217)
XLA Ops:
  0.6 68.3 %class_step.1 = (f32[1024,256]{1,0:T(8,128)}, f32[1,256]{1,0:T(1,128)}, f32[1,96]{1,0:T(1,128)}) custom-call(f32[96,4096]{1,0:T(8,128)} %images_ref.1, f32[1024,256]{1,0:T(8,128)} %source_ref.1, s32[1,256]{1,0:T(1,128)} %bitcast.5, s32[1,96]{1,0:T(1,128)} %bitcast.7, f32[1,16]{1,0:T(1,128)} %bitcast.8), custom_call_target="tpu_custom_call" | custom-call | tf_op jit(solution)/shard_map/class_step/pallas_call | solution.py:468
  69.0 0.0 copy-start
  69.0 0.0 copy-start.1
  69.0 2.3 %copy.11 = f32[1024,256]{1,0:T(8,128)} copy(f32[1024,256]{1,0:T(8,128)} %get-tuple-element.12) | data formatting | bytes 2097152
  71.3 0.0 copy-done
  71.3 0.6 copy.12
  71.8 0.0 copy-done.1
  71.8 0.5 copy.13
Async XLA Ops:
  69.0 2.3 %copy-start = (f32[1,256]{1,0:T(1,128)S(1)}, f32[1,256]{1,0:T(1,128)}, u32[]{:S(2)}) copy-start(f32[1,256]{1,0:T(1,128)} %get-tuple-element.7) | copy-start | bytes 3076
  69.0 2.8 %copy-start.1 = (f32[1,96]{1,0:T(1,128)S(1)}, f32[1,96]{1,0:T(1,128)}, u32[]{:S(2)}) copy-start(f32[1,96]{1,0:T(1,128)} %get-tuple-element.8) | copy-start | bytes 1156
